TPU v7x, 32 devices: a whole 2x2x4 slice. The times are simulated.
32 devices in a mesh: row: 8 (over z, x), col: 4 (over y, core).
Axes of the slice: x: 2, y: 2, z: 4, core: 2. Of those that a mesh axis runs over, the one named last changes fastest.
Arguments:
- points: bfloat16 [48, 1024, 1024], P('row', 'col')
- targets: bfloat16 [48, 1024, 1000], P('row', 'col'), may hold values from -6 to 6
- coeffs: float32 [48, 1024, 1000], P('row', 'col'), may hold values from -0.375 to 0.375
- block_inverse: float32 [48, 1024, 1024], P('row', 'col')
- block_order: int32 [48], replicated, may hold values from 0 to 47, each once
Outputs:
- coeffs_out: float32 [48, 1024, 1000], P('row', 'col')
All inputs are finite; a program needn't handle non-finite values.
Results may differ from a plain program's by a relative error of at most 0.0003.
Values may be sent and summed in bfloat16 or wider, within the bound.
No kernel may reach another device: no remote copies, remote signals or barrier semaphores. Data moves between devices by JAX's collectives and lax.ppermute only.
A program may use at most 128 MiB of HBM per device.

v0:
```python
import jax
import jax.numpy as jnp
from jax import lax
from jax.sharding import PartitionSpec as P

STEPS = 2
ridge_weight = 1.0


def broadcast(value, axis, source):
    kept = jnp.where(lax.axis_index(axis) == source, value, 0).astype(value.dtype)
    return lax.psum(kept, axis)


def on_device(points, targets, coeffs, block_inverse, block_order):
    blocks_here, per_col, features = points.shape
    classes = targets.shape[2]
    my_row = lax.axis_index("row")
    my_col = lax.axis_index("col")
    flat_points = points.reshape(blocks_here * per_col, features)
    flat_wide = flat_points.astype(jnp.float32)
    point_squares = jnp.sum(flat_wide * flat_wide, axis=1)
    current = coeffs
    for sweep_step in range(STEPS):
        block_id = block_order[sweep_step]
        local_index = block_id % blocks_here
        owner_row = block_id // blocks_here
        own_slice = lax.dynamic_index_in_dim(points, local_index, 0, keepdims=False)
        slice_part = broadcast(own_slice, "row", owner_row)
        active = lax.all_gather(slice_part, "col", axis=0, tiled=True)
        active_wide = active.astype(jnp.float32)
        active_squares = jnp.sum(active_wide * active_wide, axis=1)
        inner = lax.dot_general(
            active, flat_points, (((1,), (1,)), ((), ())), preferred_element_type=jnp.float32
        )
        distance = active_squares[:, None] + point_squares[None, :] - 2.0 * inner
        tile_wide = jnp.exp(-distance * (0.5 / features))
        flat_current = current.reshape(blocks_here * per_col, classes)
        products = jnp.dot(
            tile_wide,
            flat_current,
            precision=lax.Precision.HIGHEST,
            preferred_element_type=jnp.float32,
        )
        summed = lax.psum(products, ("row", "col"))
        own_sum = lax.dynamic_slice_in_dim(summed, my_col * per_col, per_col, 0)
        previous = lax.dynamic_index_in_dim(current, local_index, 0, keepdims=False)
        wanted = lax.dynamic_index_in_dim(targets, local_index, 0, keepdims=False).astype(
            jnp.float32
        )
        residual = wanted - own_sum - ridge_weight * previous
        full_residual = lax.all_gather(residual, "col", axis=0, tiled=True)
        inverse_rows = lax.dynamic_index_in_dim(block_inverse, local_index, 0, keepdims=False)
        increment = jnp.dot(
            inverse_rows,
            full_residual,
            precision=lax.Precision.HIGHEST,
            preferred_element_type=jnp.float32,
        )
        updated = jnp.where(my_row == owner_row, previous + increment, previous)
        current = lax.dynamic_update_index_in_dim(current, updated, local_index, 0)
    return current


def solution(mesh):
    placed = (
        P("row", "col", None),
        P("row", "col", None),
        P("row", "col", None),
        P("row", "col", None),
        P(),
    )
    return jax.shard_map(
        on_device, mesh=mesh, in_specs=placed, out_specs=P("row", "col", None), check_vma=False
    )
```

profile of v0, /device:TPU:0, one launch (start us, length us, event | category | flops | bytes accessed | tf_op | source)
XLA Modules:
  0.0 587.3 jit_solution(10391976789681587924)
XLA Ops:
  6.5 0.0 copy-start
  6.5 0.0 copy-start.1
  6.5 0.0 all-reduce.9.cloned.1.call-start
  6.5 6.0 %copy.15 = f32[6,256,1000]{1,2,0:T(8,128)} copy(f32[6,256,1000]{1,2,0:T(8,128)} %param.7) | data formatting | bytes 12288000
  12.5 0.0 copy-done.1
  12.5 0.6 fusion.38
  16.7 0.0 copy-done
  16.7 1.1 select_bitcast_fusion
  17.8 0.0 all-reduce.9.cloned.1.call-update
  17.8 0.0 all-gather.5.cloned.1.call-start
  17.8 81.1 %all-reduce.9.cloned.1.call-done = (bf16[256,1024]{1,0:T(8,128)(2,1)}, bf16[256,1024]{1,0:T(8,128)(2,1)}) async-done(((bf16[256,1024]{1,0:T(8,128)(2,1)}, bf16[256,1024]{1,0:T(8,128)(2,1)}), (bf16[256,1024]{1,0:T(8,128)(2,1)}, bf16[256,1024]{1,0:T(8,128)(2,1)})) %all-reduce.9.cloned.1.call-update) | async-done | bytes 1048592 | tf_op jit(solution)/shard_map/psum | solution.py:12
  98.9 0.0 all-gather.5.cloned.1.call-update
  98.9 0.0 all-reduce.5.cloned.1.call-start
  99.0 6.5 %copy.6 = f32[6,256,1000]{2,1,0:T(8,128)} copy(f32[6,256,1000]{1,2,0:T(8,128)} %copy.15) | data formatting | bytes 12288000 | tf_op args[2]
  105.5 0.7 multiply_reduce_fusion
  106.2 16.5 %all-gather.5.cloned.1.call-done = bf16[1024,1024]{1,0:T(8,128)(2,1)} async-done(((bf16[256,1024]{1,0:T(8,128)(2,1)}), bf16[1024,1024]{1,0:T(8,128)(2,1)}) %all-gather.5.cloned.1.call-update) | async-done | bytes 2097168 | tf_op jit(solution)/shard_map/all_gather | solution.py:30
  122.7 0.0 slice-start
  122.7 2.2 multiply_reduce_fusion.2
  124.9 0.0 slice-start.1
  124.9 5.2 fusion.39
  130.1 0.0 slice-done
  130.2 0.0 slice-done.1
  130.2 23.8 %fusion.7 = f32[1024,1000]{0,1:T(8,128)} fusion(f32[1536,1000]{1,0:T(8,128)S(1)} %bitcast.49, f32[1024,1536]{1,0:T(8,128)S(1)} %fusion.39, f32[1536]{0:T(1024)S(1)} %add.75, f32[1024]{0:T(1024)S(1)} %multiply_reduce_fusion.2), kind=kOutput, calls=%fused_computation.7 | convolution fusion | flops 18882232320 | bytes 16541696 | tf_op jit(solution)/shard_map/dot_general | solution.py:39
  154.0 0.0 all-reduce.5.cloned.1.call-update
  154.0 0.0 all-gather.9.cloned.1.call-start
  154.0 0.5 all-gather.9.cloned.1.call-update
  154.6 0.0 all-gather.7.cloned.1.call-start
  154.6 141.3 %all-reduce.5.cloned.1.call-done = f32[1024,1000]{0,1:T(8,128)} async-done(((f32[1024,1000]{0,1:T(8,128)}), f32[1024,1000]{0,1:T(8,128)}) %all-reduce.5.cloned.1.call-update) | async-done | bytes 4096016 | tf_op jit(solution)/shard_map/psum | solution.py:45
  295.9 2.9 fusion.31
  298.8 0.0 all-gather.7.cloned.1.call-update
  298.8 0.0 all-reduce.7.cloned.1.call-start
  298.9 2.3 constant_dynamic-slice_fusion.1
  301.1 18.6 %all-gather.9.cloned.1.call-done = bf16[1024,1024]{1,0:T(8,128)(2,1)} async-done(((bf16[256,1024]{1,0:T(8,128)(2,1)}), bf16[1024,1024]{1,0:T(8,128)(2,1)}) %all-gather.9.cloned.1.call-update) | async-done | bytes 2097168 | tf_op jit(solution)/shard_map/all_gather | solution.py:30
  319.7 2.1 multiply_reduce_fusion.1
  321.8 18.4 %fusion.40 = f32[1024,1536]{1,0:T(8,128)} fusion(bf16[1024,1024]{1,0:T(8,128)(2,1)} %all-gather.9.cloned.1.call-done, bf16[1536,1024]{1,0:T(8,128)(2,1)S(1)} %bitcast.52), kind=kOutput, calls=%fused_computation.51 | convolution fusion | flops 3221225472 | bytes 11534336 | tf_op jit(solution)/shard_map/dot_general | solution.py:33
  340.2 14.8 %all-gather.7.cloned.1.call-done = f32[1024,1000]{0,1:T(8,128)} async-done(((f32[256,1000]{0,1:T(8,128)}), f32[1024,1000]{0,1:T(8,128)}) %all-gather.7.cloned.1.call-update) | async-done | bytes 4096016 | tf_op jit(solution)/shard_map/all_gather | solution.py:52
  355.1 7.1 %fusion.25 = f32[6,256,1000]{1,2,0:T(8,128)} fusion(f32[6,256,1000]{1,2,0:T(8,128)} %copy.15, s32[]{:T(128)S(6)} %select_n.78, f32[1024,1000]{0,1:T(8,128)} %all-gather.7.cloned.1.call-done, f32[6,256,1024]{2,1,0:T(8,128)} %param.8, f32[1,256,1000]{1,2,0:T(8,128)} %constant_dynamic-slice_fusion.1, pred[]{:T(512)S(6)} %eq.11), kind=kOutput, calls=%fused_computation.30 | convolution fusion | flops 3146240000 | bytes 7194112 | tf_op jit(solution)/shard_map/dot_general | solution.py:54
  362.2 6.5 %copy.7 = f32[6,256,1000]{2,1,0:T(8,128)} copy(f32[6,256,1000]{1,2,0:T(8,128)} %fusion.25) | data formatting | bytes 12288000 | tf_op jit(solution)/shard_map/jit(dynamic_update_index_in_dim)/dynamic_update_slice | solution.py:61
  368.7 26.1 %fusion = f32[1024,1000]{0,1:T(8,128)} fusion(f32[1536,1000]{1,0:T(8,128)} %bitcast.50, f32[1024,1536]{1,0:T(8,128)} %fusion.40, f32[1024]{0:T(1024)S(1)} %multiply_reduce_fusion.1, f32[1536]{0:T(1024)S(1)} %add.75), kind=kOutput, calls=%fused_computation | convolution fusion | flops 18882232320 | bytes 16541696 | tf_op jit(solution)/shard_map/dot_general | solution.py:39
  394.8 0.0 all-reduce.7.cloned.1.call-update
  394.8 0.2 all-gather.11.cloned.1.call-start
  395.1 141.7 %all-reduce.7.cloned.1.call-done = f32[1024,1000]{0,1:T(8,128)} async-done(((f32[1024,1000]{0,1:T(8,128)}), f32[1024,1000]{0,1:T(8,128)}) %all-reduce.7.cloned.1.call-update) | async-done | bytes 4096016 | tf_op jit(solution)/shard_map/psum | solution.py:45
  536.8 2.8 fusion.30
  539.5 0.0 all-gather.11.cloned.1.call-update
  539.6 1.3 constant_dynamic-slice_fusion
  540.9 32.5 %all-gather.11.cloned.1.call-done = f32[1024,1000]{0,1:T(8,128)} async-done(((f32[256,1000]{0,1:T(8,128)}), f32[1024,1000]{0,1:T(8,128)}) %all-gather.11.cloned.1.call-update) | async-done | bytes 4096016 | tf_op jit(solution)/shard_map/all_gather | solution.py:52
  573.4 6.8 %fusion.23 = f32[6,256,1000]{1,2,0:T(8,128)} fusion(f32[6,256,1000]{1,2,0:T(8,128)} %fusion.25, s32[]{:T(128)S(6)} %select_n.87, f32[1024,1000]{0,1:T(8,128)} %all-gather.11.cloned.1.call-done, f32[6,256,1024]{2,1,0:T(8,128)} %param.8, f32[1,256,1000]{1,2,0:T(8,128)S(1)} %constant_dynamic-slice_fusion, pred[]{:T(512)S(6)} %eq.12), kind=kOutput, calls=%fused_computation.28 | convolution fusion | flops 3146240000 | bytes 7194112 | tf_op jit(solution)/shard_map/dot_general | solution.py:54
  (2 shorter events, 0.0 us)
Async XLA Ops:
  6.5 10.2 %copy-start = (bf16[6,256,1024]{2,1,0:T(8,128)(2,1)S(1)}, bf16[6,256,1024]{2,1,0:T(8,128)(2,1)}, u32[]{:S(2)}) copy-start(bf16[6,256,1024]{2,1,0:T(8,128)(2,1)} %param.5) | copy-start | bytes 9437188
  6.5 6.0 %copy-start.1 = (s32[48]{0:T(128)S(1)}, s32[48]{0:T(128)}, u32[]{:S(2)}) copy-start(s32[48]{0:T(128)} %param.9) | copy-start | bytes 580
  6.5 92.4 %all-reduce.9.cloned.1.call-start = ((), (), s32[]{:S(2)}) async-start(), calls=%async_computation.6 | async-start | bytes 2097152 | tf_op jit(solution)/shard_map/psum | solution.py:12
  17.8 104.9 %all-gather.5.cloned.1.call-start = ((), (), s32[]{:S(2)}) async-start(), calls=%async_computation | async-start | bytes 2621440 | tf_op jit(solution)/shard_map/all_gather | solution.py:30
  98.9 197.0 %all-reduce.5.cloned.1.call-start = ((), (), s32[]{:S(2)}) async-start(), calls=%async_computation.1 | async-start | bytes 8192000 | tf_op jit(solution)/shard_map/psum | solution.py:45
  122.7 7.4 %slice-start = ((s8[6291456]{0:T(1024)(128)(4,1)}), s8[4194304]{0:T(1024)(128)(4,1)S(1)}, s32[]{:S(2)}) async-start(s8[6291456]{0:T(1024)(128)(4,1)} %bitcast.47), calls=%async_computation.7 | async-start | bytes 8388608
  124.9 5.2 slice-start.1
  154.0 165.7 %all-gather.9.cloned.1.call-start = ((), (), s32[]{:S(2)}) async-start(), calls=%async_computation.3 | async-start | bytes 2621440 | tf_op jit(solution)/shard_map/all_gather | solution.py:30
  154.6 200.5 %all-gather.7.cloned.1.call-start = ((), (), s32[]{:S(2)}) async-start(), calls=%async_computation.2 | async-start | bytes 5120000 | tf_op jit(solution)/shard_map/all_gather | solution.py:52
  298.8 237.9 %all-reduce.7.cloned.1.call-start = ((), (), s32[]{:S(2)}) async-start(), calls=%async_computation.4 | async-start | bytes 8192000 | tf_op jit(solution)/shard_map/psum | solution.py:45
  394.8 178.6 %all-gather.11.cloned.1.call-start = ((), (), s32[]{:S(2)}) async-start(), calls=%async_computation.5 | async-start | bytes 5120000 | tf_op jit(solution)/shard_map/all_gather | solution.py:52
Sparse Core Ops, SparseCore 0:
  17.9 80.9 all-reduce.8
  100.5 22.1 all-gather.4
  154.1 141.7 all-reduce.4
  297.4 22.3 all-gather.8
  321.1 33.8 all-gather.6
  395.0 141.7 all-reduce.6
  539.7 33.6 all-gather.10
where the time goes:
time: 592 us; the launch traced here: 587 us
  waiting for transfers between devices  447 us (76%)
  matrix products  87.5 us (15%)
  local copies, waits for them, and re-layouts  23.2 us (4%)
  between operations  17.4 us (3%)
  other arithmetic  11.7 us (2%)
    psum x2, waiting for transfers between devices, on_device(): summed = lax.psum(products, ('row', 'col'))  283 us
    psum x1, waiting for transfers between devices, broadcast(): return lax.psum(kept, axis)  81.1 us
    dot_general x2, matrix products, on_device(): jnp.dot(tile_wide, flat_current, precision=lax.Precision.HIGHEST, preferr...  49.9 us
    all_gather x2, waiting for transfers between devices, on_device(): full_residual = lax.all_gather(residual, 'col', axis=0, tiled=True)  47.3 us
    all_gather x2, waiting for transfers between devices, on_device(): active = lax.all_gather(slice_part, 'col', axis=0, tiled=True)  35.1 us
    dot_general x2, matrix products, on_device(): lax.dot_general(active, flat_points, (((1,), (1,)), ((), ())), preferred_...  23.6 us
    dot_general x2, matrix products, on_device(): jnp.dot(inverse_rows, full_residual, precision=lax.Precision.HIGHEST, pre...  13.9 us
    unnamed x10, local copies, waits for them, and re-layouts  12.5 us
  transfers between devices with their start and end apart: 7, of which 7 were waited for; matrix products, arithmetic and copies ran while one was open for 6% of the time, Pallas kernels for 0%

commit v1 on v0

--- a/solution.py
+++ b/solution.py
@@ -42,7 +42,7 @@
             precision=lax.Precision.HIGHEST,
             preferred_element_type=jnp.float32,
         )
-        summed = lax.psum(products, ("row", "col"))
+        summed = lax.psum(lax.psum(products, "col"), "row")
         own_sum = lax.dynamic_slice_in_dim(summed, my_col * per_col, per_col, 0)
         previous = lax.dynamic_index_in_dim(current, local_index, 0, keepdims=False)
         wanted = lax.dynamic_index_in_dim(targets, local_index, 0, keepdims=False).astype(

time: 592 us -> 790 us (1.33)
  waiting for transfers between devices: 447 us -> 645 us
    psum x2 -> x4, waiting for transfers between devices: 283 us -> 482 us  [on_device(): summed = lax.psum(lax.psum(products, 'col'), 'row')]
  transfers between devices with their start and end apart: 7 -> 9, of which waited for: 7 -> 9; matrix products, arithmetic and copies ran while one was open for 6% -> 4% of each run, Pallas kernels for 0% -> 0%
where the time goes in v1:
time: 790 us; the launch traced here: 785 us
  waiting for transfers between devices  645 us (82%)
  matrix products  87.5 us (11%)
  local copies, waits for them, and re-layouts  23.2 us (3%)
  between operations  17.1 us (2%)
  other arithmetic  11.7 us (1%)
    psum x4, waiting for transfers between devices, on_device(): summed = lax.psum(lax.psum(products, 'col'), 'row')  482 us
    psum x1, waiting for transfers between devices, broadcast(): return lax.psum(kept, axis)  81.1 us
    dot_general x2, matrix products, on_device(): jnp.dot(tile_wide, flat_current, precision=lax.Precision.HIGHEST, preferr...  49.9 us
    all_gather x2, waiting for transfers between devices, on_device(): full_residual = lax.all_gather(residual, 'col', axis=0, tiled=True)  46.6 us
    all_gather x2, waiting for transfers between devices, on_device(): active = lax.all_gather(slice_part, 'col', axis=0, tiled=True)  34.3 us
    dot_general x2, matrix products, on_device(): lax.dot_general(active, flat_points, (((1,), (1,)), ((), ())), preferred_...  23.7 us
  transfers between devices with their start and end apart: 9, of which 9 were waited for; matrix products, arithmetic and copies ran while one was open for 4% of the time, Pallas kernels for 0%

profile of v1, /device:TPU:0, one launch (start us, length us, event | category | flops | bytes accessed | tf_op | source)
XLA Modules:
  0.0 785.0 jit_solution(9437434270645593975)
XLA Ops:
  6.5 0.0 copy-start
  6.5 0.0 copy-start.1
  6.5 0.0 all-reduce.15.cloned.1.call-start
  6.5 6.0 copy.17
  12.5 0.0 copy-done.1
  12.5 0.6 fusion.38
  16.7 0.0 copy-done
  16.7 1.1 select_bitcast_fusion
  17.8 0.0 all-reduce.15.cloned.1.call-update
  17.8 0.0 all-gather.5.cloned.1.call-start
  17.8 81.1 %all-reduce.15.cloned.1.call-done = (bf16[256,1024]{1,0:T(8,128)(2,1)}, bf16[256,1024]{1,0:T(8,128)(2,1)}) async-done(((bf16[256,1024]{1,0:T(8,128)(2,1)}, bf16[256,1024]{1,0:T(8,128)(2,1)}), (bf16[256,1024]{1,0:T(8,128)(2,1)}, bf16[256,1024]{1,0:T(8,128)(2,1)})) %all-reduce.15.cloned.1.call-update) | async-done | bytes 1048592 | tf_op jit(solution)/shard_map/psum | solution.py:12
  98.9 0.0 all-gather.5.cloned.1.call-update
  98.9 0.0 all-reduce.7.cloned.1.call-start
  99.0 6.5 copy.6
  105.5 0.7 multiply_reduce_fusion
  106.2 16.5 %all-gather.5.cloned.1.call-done = bf16[1024,1024]{1,0:T(8,128)(2,1)} async-done(((bf16[256,1024]{1,0:T(8,128)(2,1)}), bf16[1024,1024]{1,0:T(8,128)(2,1)}) %all-gather.5.cloned.1.call-update) | async-done | bytes 2097168 | tf_op jit(solution)/shard_map/all_gather | solution.py:30
  122.7 0.0 slice-start
  122.7 2.2 multiply_reduce_fusion.2
  124.9 0.0 slice-start.1
  124.9 5.2 fusion.39
  130.1 0.0 slice-done
  130.2 0.0 slice-done.1
  130.2 23.8 %fusion.7 = f32[1024,1000]{0,1:T(8,128)} fusion(f32[1536,1000]{1,0:T(8,128)S(1)} %bitcast.49, f32[1024,1536]{1,0:T(8,128)S(1)} %fusion.39, f32[1536]{0:T(1024)S(1)} %add.79, f32[1024]{0:T(1024)S(1)} %multiply_reduce_fusion.2), kind=kOutput, calls=%fused_computation.7 | convolution fusion | flops 18882232320 | bytes 16541696 | tf_op jit(solution)/shard_map/dot_general | solution.py:39
  154.0 0.0 all-reduce.7.cloned.1.call-update
  154.0 0.0 all-reduce.9.cloned.1.call-start
  154.0 84.0 %all-reduce.7.cloned.1.call-done = f32[1024,1000]{0,1:T(8,128)} async-done(((f32[1024,1000]{0,1:T(8,128)}), f32[1024,1000]{0,1:T(8,128)}) %all-reduce.7.cloned.1.call-update) | async-done | bytes 4096016 | tf_op jit(solution)/shard_map/psum | solution.py:45
  238.0 0.0 all-reduce.9.cloned.1.call-update
  238.1 0.0 all-gather.9.cloned.1.call-start
  238.1 0.5 all-gather.9.cloned.1.call-update
  238.7 0.0 all-gather.7.cloned.1.call-start
  238.7 156.9 %all-reduce.9.cloned.1.call-done = f32[1024,1000]{0,1:T(8,128)} async-done(((f32[1024,1000]{0,1:T(8,128)}), f32[1024,1000]{0,1:T(8,128)}) %all-reduce.9.cloned.1.call-update) | async-done | bytes 4096016 | tf_op jit(solution)/shard_map/psum | solution.py:45
  395.6 2.9 fusion.31
  398.4 0.0 all-gather.7.cloned.1.call-update
  398.5 0.0 all-reduce.11.cloned.1.call-start
  398.5 2.3 constant_dynamic-slice_fusion.1
  400.8 17.8 %all-gather.9.cloned.1.call-done = bf16[1024,1024]{1,0:T(8,128)(2,1)} async-done(((bf16[256,1024]{1,0:T(8,128)(2,1)}), bf16[1024,1024]{1,0:T(8,128)(2,1)}) %all-gather.9.cloned.1.call-update) | async-done | bytes 2097168 | tf_op jit(solution)/shard_map/all_gather | solution.py:30
  418.6 2.1 multiply_reduce_fusion.1
  420.7 18.5 %fusion.40 = f32[1024,1536]{1,0:T(8,128)} fusion(bf16[1024,1024]{1,0:T(8,128)(2,1)} %all-gather.9.cloned.1.call-done, bf16[1536,1024]{1,0:T(8,128)(2,1)S(1)} %bitcast.52), kind=kOutput, calls=%fused_computation.51 | convolution fusion | flops 3221225472 | bytes 11534336 | tf_op jit(solution)/shard_map/dot_general | solution.py:33
  439.1 14.8 %all-gather.7.cloned.1.call-done = f32[1024,1000]{0,1:T(8,128)} async-done(((f32[256,1000]{0,1:T(8,128)}), f32[1024,1000]{0,1:T(8,128)}) %all-gather.7.cloned.1.call-update) | async-done | bytes 4096016 | tf_op jit(solution)/shard_map/all_gather | solution.py:52
  453.9 7.1 fusion.25
  461.0 6.5 copy.7
  467.5 26.1 %fusion = f32[1024,1000]{0,1:T(8,128)} fusion(f32[1536,1000]{1,0:T(8,128)} %bitcast.50, f32[1024,1536]{1,0:T(8,128)} %fusion.40, f32[1024]{0:T(1024)S(1)} %multiply_reduce_fusion.1, f32[1536]{0:T(1024)S(1)} %add.79), kind=kOutput, calls=%fused_computation | convolution fusion | flops 18882232320 | bytes 16541696 | tf_op jit(solution)/shard_map/dot_general | solution.py:39
  493.7 0.0 all-reduce.11.cloned.1.call-update
  493.7 0.0 all-reduce.13.cloned.1.call-start
  493.8 84.0 %all-reduce.11.cloned.1.call-done = f32[1024,1000]{0,1:T(8,128)} async-done(((f32[1024,1000]{0,1:T(8,128)}), f32[1024,1000]{0,1:T(8,128)}) %all-reduce.11.cloned.1.call-update) | async-done | bytes 4096016 | tf_op jit(solution)/shard_map/psum | solution.py:45
  577.8 0.0 all-reduce.13.cloned.1.call-update
  577.8 0.2 all-gather.11.cloned.1.call-start
  578.0 157.4 %all-reduce.13.cloned.1.call-done = f32[1024,1000]{0,1:T(8,128)} async-done(((f32[1024,1000]{0,1:T(8,128)}), f32[1024,1000]{0,1:T(8,128)}) %all-reduce.13.cloned.1.call-update) | async-done | bytes 4096016 | tf_op jit(solution)/shard_map/psum | solution.py:45
  735.5 2.9 fusion.30
  738.3 0.0 all-gather.11.cloned.1.call-update
  738.4 1.3 constant_dynamic-slice_fusion
  739.7 31.8 %all-gather.11.cloned.1.call-done = f32[1024,1000]{0,1:T(8,128)} async-done(((f32[256,1000]{0,1:T(8,128)}), f32[1024,1000]{0,1:T(8,128)}) %all-gather.11.cloned.1.call-update) | async-done | bytes 4096016 | tf_op jit(solution)/shard_map/all_gather | solution.py:52
  771.4 6.8 fusion.23
  (2 shorter events, 0.0 us)
Async XLA Ops:
  6.5 10.2 %copy-start = (bf16[6,256,1024]{2,1,0:T(8,128)(2,1)S(1)}, bf16[6,256,1024]{2,1,0:T(8,128)(2,1)}, u32[]{:S(2)}) copy-start(bf16[6,256,1024]{2,1,0:T(8,128)(2,1)} %param.5) | copy-start | bytes 9437188
  6.5 6.0 copy-start.1
  6.5 92.4 %all-reduce.15.cloned.1.call-start = ((), (), s32[]{:S(2)}) async-start(), calls=%async_computation.8 | async-start | bytes 2097152 | tf_op jit(solution)/shard_map/psum | solution.py:12
  17.8 104.9 %all-gather.5.cloned.1.call-start = ((), (), s32[]{:S(2)}) async-start(), calls=%async_computation | async-start | bytes 2621440 | tf_op jit(solution)/shard_map/all_gather | solution.py:30
  98.9 139.1 %all-reduce.7.cloned.1.call-start = ((), (), s32[]{:S(2)}) async-start(), calls=%async_computation.1 | async-start | bytes 8192000 | tf_op jit(solution)/shard_map/psum | solution.py:45
  122.7 7.4 slice-start
  124.9 5.2 slice-start.1
  154.0 241.6 %all-reduce.9.cloned.1.call-start = ((), (), s32[]{:S(2)}) async-start(), calls=%async_computation.2 | async-start | bytes 8192000 | tf_op jit(solution)/shard_map/psum | solution.py:45
  238.1 180.5 %all-gather.9.cloned.1.call-start = ((), (), s32[]{:S(2)}) async-start(), calls=%async_computation.4 | async-start | bytes 2621440 | tf_op jit(solution)/shard_map/all_gather | solution.py:30
  238.7 215.3 %all-gather.7.cloned.1.call-start = ((), (), s32[]{:S(2)}) async-start(), calls=%async_computation.3 | async-start | bytes 5120000 | tf_op jit(solution)/shard_map/all_gather | solution.py:52
  398.5 179.3 %all-reduce.11.cloned.1.call-start = ((), (), s32[]{:S(2)}) async-start(), calls=%async_computation.5 | async-start | bytes 8192000 | tf_op jit(solution)/shard_map/psum | solution.py:45
  493.7 241.7 %all-reduce.13.cloned.1.call-start = ((), (), s32[]{:S(2)}) async-start(), calls=%async_computation.6 | async-start | bytes 8192000 | tf_op jit(solution)/shard_map/psum | solution.py:45
  577.8 193.6 %all-gather.11.cloned.1.call-start = ((), (), s32[]{:S(2)}) async-start(), calls=%async_computation.7 | async-start | bytes 5120000 | tf_op jit(solution)/shard_map/all_gather | solution.py:52
Sparse Core Ops, SparseCore 0:
  17.9 80.9 all-reduce.14
  100.5 22.1 all-gather.4
  154.1 83.8 all-reduce.6
  241.6 153.9 all-reduce.8
  397.0 21.5 all-gather.8
  420.0 33.8 all-gather.6
  493.8 83.8 all-reduce.10
  581.4 153.9 all-reduce.12
  738.5 32.9 all-gather.10
